TPU v7x, 32 devices: a whole 2x2x4 slice. The times are simulated.
32 devices in a mesh: ray: 16 (over z, x, core), vox: 2 (over y).
Axes of the slice: x: 2, y: 2, z: 4, core: 2. Of those that a mesh axis runs over, the one named last changes fastest.
Arguments:
- tiles: bfloat16 [16, 2, 32, 128, 128], P('ray', 'vox'), may hold values from -0.1875 to 0.1875
- tile_scale: float32 [16, 2, 32], P('ray', 'vox'), may hold values from 0.25 to 4
- tile_row: int32 [16, 2, 32], P('ray', 'vox'), may hold values from 0 to 7
- tile_col: int32 [16, 2, 32], P('ray', 'vox'), may hold values from 0 to 1023
- tile_count: int32 [16, 2], P('ray', 'vox'), may hold values from 16 to 32, as said below
- delays: float32 [16384], P('ray'), may hold values from -6 to 6
- ray_receiver: int32 [16384], P('ray'), may hold values from 0 to 95
- receiver_weight: float32 [1536], P('ray'), may hold values from 0.5 to 2
- smooth_scale: float32 [64], replicated, may hold values from 0.05 to 0.5
Outputs:
- density: float32 [64, 2, 16, 128], P('ray', None, 'vox')
- rays_vec: float32 [16384], P('ray')
Inputs may be any that keep to these rules, and one draw needn't show every extreme that they name: `tile_count`: each ray group and voxel slab has between 16 and 32 live tile slots, and some has all 32 in every draw.
All inputs are finite; a program needn't handle non-finite values.
Results may differ from a plain program's by a relative error of at most 0.013.
Values sent between devices are 32-bit elements; how exact they have to be, the bound alone decides.
No kernel may reach another device: no remote copies, remote signals or barrier semaphores. Data moves between devices by JAX's collectives and lax.ppermute only.
A program may use at most 64 MiB of HBM per device.

v0:
```python
import jax
import jax.numpy as jnp
from jax import lax
from jax.sharding import PartitionSpec as P

ALT = 64
EPOCHS = 2
LAT = 128
LON_DEV = 8
RAY_TILE = 128
RT = 8
ITERS = 2
LATERAL = 1.0
VERTICAL = 4.0
TEMPORAL = 0.5


def with_halo(block, sides, width):
    for axis, dim in sides:
        count = lax.axis_size(axis)
        forward = [(i, i + 1) for i in range(count - 1)]
        backward = [(target, source) for source, target in forward]
        low = lax.ppermute(
            lax.slice_in_dim(block, block.shape[dim] - width, None, axis=dim), axis, forward
        )
        high = lax.ppermute(lax.slice_in_dim(block, 0, width, axis=dim), axis, backward)
        block = jnp.concatenate([low, block, high], axis=dim)
    return block


def stencil(padded, field):
    lateral = padded[1:-1, 1:-1, 2:, 1:-1] + padded[1:-1, 1:-1, :-2, 1:-1]
    lateral = lateral + padded[1:-1, 1:-1, 1:-1, 2:] + padded[1:-1, 1:-1, 1:-1, :-2]
    vertical = padded[2:, 1:-1, 1:-1, 1:-1] + padded[:-2, 1:-1, 1:-1, 1:-1]
    temporal = padded[1:-1, 2:, 1:-1, 1:-1] + padded[1:-1, :-2, 1:-1, 1:-1]
    centre = 2.0 * (2.0 * LATERAL + VERTICAL + TEMPORAL)
    return centre * field - LATERAL * lateral - VERTICAL * vertical - TEMPORAL * temporal


def laplace_local(field):
    padded = with_halo(field, (("vox", 2),), 1)
    padded = jnp.pad(padded, ((1, 1), (1, 1), (0, 0), (1, 1)))
    return stencil(padded, field)


def on_device(
    tiles,
    tile_scale,
    tile_row,
    tile_col,
    tile_count,
    delays,
    ray_receiver,
    receiver_weight,
    smooth_scale,
):
    block = tiles[0, 0]
    row_index = tile_row[0, 0]
    col_index = tile_col[0, 0]
    slots = block.shape[0]
    live = (jnp.arange(slots) < tile_count[0, 0]).astype(jnp.float32)
    effective = tile_scale[0, 0] * live
    table_size = receiver_weight.shape[0]
    matches = ray_receiver[:, None] == jnp.arange(table_size)[None, :]
    ray_weight = jnp.sum(jnp.where(matches, receiver_weight[None, :], 0.0), axis=1)
    damping = smooth_scale[:, None, None, None]
    lines_total = ALT * EPOCHS * LON_DEV
    share_rows = ALT // lax.axis_size("ray")
    offset = lax.axis_index("ray") * share_rows
    ray_onehot = (row_index[None, :] == jnp.arange(RT)[:, None]).astype(jnp.float32)

    def ray_total(values):
        return lax.psum(jnp.sum(values * values), "ray")

    def slab_total(values):
        return lax.psum(jnp.sum(values * values), "vox")

    def adjoint_lines(weighted):
        picked = jnp.take(weighted.reshape(RT, RAY_TILE), row_index, axis=0)
        return (
            jnp.einsum("ktl,kt->kl", block, picked, preferred_element_type=jnp.float32)
            * effective[:, None]
        )

    def pull_back(weighted):
        contrib = adjoint_lines(weighted)
        onehot = (col_index[None, :] == jnp.arange(lines_total)[:, None]).astype(jnp.float32)
        summed = jnp.dot(onehot, contrib, precision=lax.Precision.HIGHEST).reshape(
            ALT, EPOCHS, LON_DEV, LAT
        )
        return lax.psum(summed, "ray")

    def right_norm_of(values):
        return jnp.sqrt(slab_total(values))

    rays_vec = ray_weight * delays
    left_norm = jnp.sqrt(ray_total(rays_vec))
    rays_vec = rays_vec / left_norm
    smooth_vec = jnp.zeros((ALT, EPOCHS, LON_DEV, LAT), jnp.float32)
    right = pull_back((ray_weight * rays_vec).astype(jnp.bfloat16))
    right_norm = right_norm_of(right)
    right = right / right_norm
    search = right
    density = jnp.zeros_like(right)
    resid_bar = left_norm
    diag_bar = right_norm
    for iteration in range(ITERS):
        current = right
        smooth_vec = damping * laplace_local(current) - right_norm * smooth_vec
        lines = current.reshape(lines_total, LAT).astype(jnp.bfloat16)
        forward_picked = jnp.take(lines, col_index, axis=0)
        rays = (
            jnp.einsum("ktl,kl->kt", block, forward_picked, preferred_element_type=jnp.float32)
            * effective[:, None]
        )
        partial_value = jnp.dot(ray_onehot, rays, precision=lax.Precision.HIGHEST).reshape(-1)
        ray_sums = lax.psum(partial_value, "vox")
        smooth_sq = slab_total(smooth_vec)
        rays_vec = ray_weight * ray_sums - right_norm * rays_vec
        left_norm = jnp.sqrt(ray_total(rays_vec) + smooth_sq)
        rays_vec = rays_vec / left_norm
        smooth_vec = smooth_vec / left_norm
        smoothing = laplace_local(damping * smooth_vec)
        right = (
            pull_back((ray_weight * rays_vec).astype(jnp.bfloat16)) + smoothing - left_norm * right
        )
        right_norm = right_norm_of(right)
        right = right / right_norm
        diag_new = jnp.sqrt(diag_bar * diag_bar + left_norm * left_norm)
        cosine = diag_bar / diag_new
        sine_value = left_norm / diag_new
        coupling = sine_value * right_norm
        diag_bar = -cosine * right_norm
        step_size = cosine * resid_bar
        resid_bar = sine_value * resid_bar
        density = density + step_size / diag_new * search
        search = right - coupling / diag_new * search
    density_out = lax.dynamic_slice_in_dim(density, offset, share_rows, 0)
    return (density_out, rays_vec)


def solution(mesh):
    in_specs = (
        P("ray", "vox", None, None, None),
        P("ray", "vox", None),
        P("ray", "vox", None),
        P("ray", "vox", None),
        P("ray", "vox"),
        P("ray"),
        P("ray"),
        P("ray"),
        P(),
    )
    out_specs = (P("ray", None, "vox", None), P("ray"))
    return jax.shard_map(
        on_device, mesh=mesh, in_specs=in_specs, out_specs=out_specs, check_vma=False
    )
```

profile of v0, /device:TPU:0, one launch (start us, length us, event | category | flops | bytes accessed | tf_op | source)
XLA Modules:
  0.0 363.2 jit_solution(5082143402132900104)
XLA Ops:
  7.2 0.7 compare_select_fusion.1
  8.0 0.7 compare_and_fusion.1
  8.6 0.8 select_reduce_fusion
  9.5 1.3 multiply_reduce_fusion.5
  10.8 35.5 %psum.77 = f32[]{:T(128)} all-reduce(f32[]{:T(128)} %get-tuple-element.20), channel_id=1, replica_groups=mesh['ray'=16,'vox'=2] {'ray'}, use_global_device_ids=true, to_apply=%region_2.3 | all-reduce | flops 1 | bytes 8 | tf_op jit(solution)/shard_map/psum | solution.py:73
  48.7 0.7 compare_select_fusion.2
  49.4 1.9 fusion.40
  51.3 0.7 compare_select_fusion
  52.0 0.7 compare_and_fusion
  52.7 86.1 %all-reduce.8.cloned.1.call-done = f32[64,2,8,128]{3,2,1,0:T(8,128)} async-done(((f32[64,2,8,128]{3,2,1,0:T(8,128)}), f32[64,2,8,128]{3,2,1,0:T(8,128)}) %all-reduce.8.cloned.1.call-update) | async-done | bytes 524304 | tf_op jit(solution)/shard_map/psum | solution.py:91
  138.7 1.8 multiply_reduce_fusion.2
  140.5 5.5 %psum.79 = f32[]{:T(128)} all-reduce(f32[]{:T(128)} %multiply_reduce_fusion.2), channel_id=1, replica_groups=mesh['ray'=16,'vox'=2] {'vox'}, use_global_device_ids=true, to_apply=%region_5.7 | all-reduce | flops 1 | bytes 8 | tf_op jit(solution)/shard_map/psum | solution.py:76
  146.7 1.1 fusion.64
  148.0 1.3 collective-permute-start
  149.3 4.5 %collective-permute-start.1 = (f32[64,2,1,128]{3,2,1,0:T(1,128)S(1)}, f32[64,2,1,128]{3,2,1,0:T(1,128)S(1)}, u32[]{:S(2)}, u32[]{:S(2)}) collective-permute-start(f32[64,2,1,128]{3,2,1,0:T(1,128)S(1)} %get-tuple-element.26), channel_id=1, source_target_pairs={{0,1},{2,3},{4,5},{6,7},{8,9},{10,11},{12,13},{14,15},{16,17},{18,... | collective-permute-start | bytes 196616 | tf_op jit(solution)/shard_map/ppermute | solution.py:23
  155.7 2.4 select_maximum_fusion.4
  158.1 1.5 multiply_reduce_fusion.1
  159.6 5.9 %all-reduce.4 = (f32[1024]{0:T(1024)S(1)}, f32[]{:T(128)}) all-reduce(f32[1024]{0:T(1024)S(1)} %convolution_bitcast_fusion.1, f32[]{:T(128)} %get-tuple-element.16), channel_id=1, replica_groups=mesh['ray'=16,'vox'=2] {'vox'}, use_global_device_ids=true, to_apply=%region_6.9 | all-reduce | flops 1025 | bytes 8200 | tf_op jit(solution)/shard_map/psum | solution.py:117
  166.2 30.1 %psum.81 = f32[]{:T(128)} all-reduce(f32[]{:T(128)} %get-tuple-element.14), channel_id=1, replica_groups=mesh['ray'=16,'vox'=2] {'ray'}, use_global_device_ids=true, to_apply=%region_8.11 | all-reduce | flops 1 | bytes 8 | tf_op jit(solution)/shard_map/psum | solution.py:73
  197.8 1.3 collective-permute-start.2
  199.1 4.5 %collective-permute-start.3 = (f32[64,2,1,128]{3,2,1,0:T(1,128)S(1)}, f32[64,2,1,128]{3,2,1,0:T(1,128)S(1)}, u32[]{:S(2)}, u32[]{:S(2)}) collective-permute-start(f32[64,2,1,128]{3,2,1,0:T(1,128)S(1)} %get-tuple-element.24), channel_id=1, source_target_pairs={{0,1},{2,3},{4,5},{6,7},{8,9},{10,11},{12,13},{14,15},{16,17},{18,... | collective-permute-start | bytes 196616 | tf_op jit(solution)/shard_map/ppermute | solution.py:23
  204.8 1.2 fusion.39
  206.2 3.7 %select_maximum_fusion.2 = f32[66,4,10,130]{3,2,1,0:T(8,128)} fusion(f32[64,2,1,128]{3,2,1,0:T(1,128)S(1)} %collective-permute-done.2, f32[64,2,8,128]{3,2,1,0:T(8,128)S(1)} %broadcast_multiply_fusion, f32[64,2,1,128]{3,2,1,0:T(1,128)S(1)} %collective-permute-done.3), kind=kLoop, calls=%fused_computation.12 | loop fusion | flops 7550400 | bytes 2028160 | tf_op jit(solution)/shard_map/concatenate | solution.py:27
  210.0 82.2 %all-reduce.10.cloned.1.call-done = f32[64,2,8,128]{3,2,1,0:T(8,128)} async-done(((f32[64,2,8,128]{3,2,1,0:T(8,128)}), f32[64,2,8,128]{3,2,1,0:T(8,128)}) %all-reduce.10.cloned.1.call-update) | async-done | bytes 524304 | tf_op jit(solution)/shard_map/psum | solution.py:91
  292.2 6.6 %multiply_reduce_fusion = (f32[]{:T(128)}, f32[64,2,8,128]{3,2,1,0:T(8,128)S(1)}) fusion(f32[64,2,8,128]{3,2,1,0:T(8,128)S(1)} %get-tuple-element.19, f32[]{:T(128)S(6)} %sqrt.23, f32[64,2,8,128]{3,2,1,0:T(8,128)} %all-reduce.10.cloned.1.call-done, f32[66,4,10,130]{3,2,1,0:T(8,128)} %select_maximum_fusion.2, ...), kind=kLoop, calls=%fused_computation.75 | loop fusion | flops 2359295 | bytes 5373960 | tf_op jit(solution)/shard_map/reduce_sum | solution.py:76
  298.9 5.5 %psum.84 = f32[]{:T(128)} all-reduce(f32[]{:T(128)} %get-tuple-element.12), channel_id=1, replica_groups=mesh['ray'=16,'vox'=2] {'vox'}, use_global_device_ids=true, to_apply=%region_13.16 | all-reduce | flops 1 | bytes 8 | tf_op jit(solution)/shard_map/psum | solution.py:76
  305.3 1.3 collective-permute-start.4
  306.6 4.5 %collective-permute-start.5 = (f32[64,2,1,128]{3,2,1,0:T(1,128)S(1)}, f32[64,2,1,128]{3,2,1,0:T(1,128)S(1)}, u32[]{:S(2)}, u32[]{:S(2)}) collective-permute-start(f32[64,2,1,128]{3,2,1,0:T(1,128)S(1)} %get-tuple-element.22), channel_id=1, source_target_pairs={{0,1},{2,3},{4,5},{6,7},{8,9},{10,11},{12,13},{14,15},{16,17},{18,... | collective-permute-start | bytes 196616 | tf_op jit(solution)/shard_map/ppermute | solution.py:23
  313.0 2.4 select_maximum_fusion
  315.4 1.6 fusion.18
  317.0 5.9 %all-reduce.3 = (f32[1024]{0:T(1024)S(1)}, f32[]{:T(128)}) all-reduce(f32[1024]{0:T(1024)S(1)} %convolution_bitcast_fusion, f32[]{:T(128)} %fusion.18), channel_id=1, replica_groups=mesh['ray'=16,'vox'=2] {'vox'}, use_global_device_ids=true, to_apply=%region_14.17 | all-reduce | flops 1025 | bytes 8200 | tf_op jit(solution)/shard_map/psum | solution.py:117
  323.5 30.1 %psum.86 = f32[]{:T(128)} all-reduce(f32[]{:T(128)} %get-tuple-element.8), channel_id=1, replica_groups=mesh['ray'=16,'vox'=2] {'ray'}, use_global_device_ids=true, to_apply=%region_16.19 | all-reduce | flops 1 | bytes 8 | tf_op jit(solution)/shard_map/psum | solution.py:73
  (45 shorter events, 8.9 us)
Async XLA Ops:
  7.2 41.1 %copy-start = (bf16[1,1,32,128,128]{4,3,2,1,0:T(8,128)(2,1)S(1)}, bf16[1,1,32,128,128]{4,3,2,1,0:T(8,128)(2,1)}, u32[]{:S(2)}) copy-start(bf16[1,1,32,128,128]{4,3,2,1,0:T(8,128)(2,1)} %param.13) | copy-start | bytes 3145732
  7.2 148.0 %copy-start.3 = (s32[1,1,32]{2,1,0:T(1,128)S(1)}, s32[1,1,32]{2,1,0:T(1,128)}, u32[]{:S(2)}) copy-start(s32[1,1,32]{2,1,0:T(1,128)} %param.15) | copy-start | bytes 388
  7.2 131.5 %all-reduce.8.cloned.1.call-start = ((), (), s32[]{:S(2)}) async-start(), calls=%async_computation | async-start | bytes 1048576 | tf_op jit(solution)/shard_map/psum | solution.py:91
  51.3 106.8 %copy-start.1 = (f32[64]{0:T(128)S(1)}, f32[64]{0:T(128)}, u32[]{:S(2)}) copy-start(f32[64]{0:T(128)} %param.21) | copy-start | bytes 772
  51.3 240.9 %all-reduce.10.cloned.1.call-start = ((), (), s32[]{:S(2)}) async-start(), calls=%async_computation.1 | async-start | bytes 1048576 | tf_op jit(solution)/shard_map/psum | solution.py:91
  148.0 7.4 %collective-permute-start = (f32[64,2,1,128]{3,2,1,0:T(1,128)S(1)}, f32[64,2,1,128]{3,2,1,0:T(1,128)S(1)}, u32[]{:S(2)}, u32[]{:S(2)}) collective-permute-start(f32[64,2,1,128]{3,2,1,0:T(1,128)S(1)} %get-tuple-element.27), channel_id=1, source_target_pairs={{1,0},{3,2},{5,4},{7,6},{9,8},{11,10},{13,12},{15,14},{17,16},{19,... | collective-permute-start | bytes 196616 | tf_op jit(solution)/shard_map/ppermute | solution.py:26
  149.3 6.4 %collective-permute-start.1 = (f32[64,2,1,128]{3,2,1,0:T(1,128)S(1)}, f32[64,2,1,128]{3,2,1,0:T(1,128)S(1)}, u32[]{:S(2)}, u32[]{:S(2)}) collective-permute-start(f32[64,2,1,128]{3,2,1,0:T(1,128)S(1)} %get-tuple-element.26), channel_id=1, source_target_pairs={{0,1},{2,3},{4,5},{6,7},{8,9},{10,11},{12,13},{14,15},{16,17},{18,... | collective-permute-start | bytes 196616 | tf_op jit(solution)/shard_map/ppermute | solution.py:23
  158.1 46.7 %copy-start.2 = (s32[1,1,32]{2,1,0:T(1,128)S(1)}, s32[1,1,32]{2,1,0:T(1,128)}, u32[]{:S(2)}) copy-start(s32[1,1,32]{2,1,0:T(1,128)} %param.16) | copy-start | bytes 388
  197.8 8.4 %collective-permute-start.2 = (f32[64,2,1,128]{3,2,1,0:T(1,128)S(1)}, f32[64,2,1,128]{3,2,1,0:T(1,128)S(1)}, u32[]{:S(2)}, u32[]{:S(2)}) collective-permute-start(f32[64,2,1,128]{3,2,1,0:T(1,128)S(1)} %get-tuple-element.25), channel_id=1, source_target_pairs={{1,0},{3,2},{5,4},{7,6},{9,8},{11,10},{13,12},{15,14},{17,16},{19,... | collective-permute-start | bytes 196616 | tf_op jit(solution)/shard_map/ppermute | solution.py:26
  199.1 7.1 %collective-permute-start.3 = (f32[64,2,1,128]{3,2,1,0:T(1,128)S(1)}, f32[64,2,1,128]{3,2,1,0:T(1,128)S(1)}, u32[]{:S(2)}, u32[]{:S(2)}) collective-permute-start(f32[64,2,1,128]{3,2,1,0:T(1,128)S(1)} %get-tuple-element.24), channel_id=1, source_target_pairs={{0,1},{2,3},{4,5},{6,7},{8,9},{10,11},{12,13},{14,15},{16,17},{18,... | collective-permute-start | bytes 196616 | tf_op jit(solution)/shard_map/ppermute | solution.py:23
  305.3 7.4 %collective-permute-start.4 = (f32[64,2,1,128]{3,2,1,0:T(1,128)S(1)}, f32[64,2,1,128]{3,2,1,0:T(1,128)S(1)}, u32[]{:S(2)}, u32[]{:S(2)}) collective-permute-start(f32[64,2,1,128]{3,2,1,0:T(1,128)S(1)} %get-tuple-element.23), channel_id=1, source_target_pairs={{1,0},{3,2},{5,4},{7,6},{9,8},{11,10},{13,12},{15,14},{17,16},{19,... | collective-permute-start | bytes 196616 | tf_op jit(solution)/shard_map/ppermute | solution.py:26
  306.6 6.4 %collective-permute-start.5 = (f32[64,2,1,128]{3,2,1,0:T(1,128)S(1)}, f32[64,2,1,128]{3,2,1,0:T(1,128)S(1)}, u32[]{:S(2)}, u32[]{:S(2)}) collective-permute-start(f32[64,2,1,128]{3,2,1,0:T(1,128)S(1)} %get-tuple-element.22), channel_id=1, source_target_pairs={{0,1},{2,3},{4,5},{6,7},{8,9},{10,11},{12,13},{14,15},{16,17},{18,... | collective-permute-start | bytes 196616 | tf_op jit(solution)/shard_map/ppermute | solution.py:23
Sparse Core Ops, SparseCore 0:
  51.4 87.2 all-reduce.7
  206.3 85.8 all-reduce.9
where the time goes:
time: 364 us; the launch traced here: 363 us
  waiting for transfers between devices  169 us (46%)
  blocking collectives  119 us (33%)
  other arithmetic  29.7 us (8%)
  between operations  20 us (5%)
  starting transfers between devices  17.6 us (5%)
  matrix products  5.56 us (2%)
    psum x2, waiting for transfers between devices, pull_back(): return lax.psum(summed, 'ray')  168 us
    psum x3, blocking collectives, ray_total(): return lax.psum(jnp.sum(values * values), 'ray')  95.7 us
    ppermute x3, starting transfers between devices, with_halo(): lax.ppermute(lax.slice_in_dim(block, block.shape[dim] - width, None, axis...  13.6 us
    psum x2, blocking collectives, on_device(): ray_sums = lax.psum(partial_value, 'vox')  11.9 us
    reduce_sum x4, other arithmetic, slab_total(): return lax.psum(jnp.sum(values * values), 'vox')  11.6 us
    psum x2, blocking collectives, slab_total(): return lax.psum(jnp.sum(values * values), 'vox')  11.1 us
    concatenate x3, other arithmetic, with_halo(): block = jnp.concatenate([low, block, high], axis=dim)  8.48 us
  transfers between devices with their start and end apart: 8, of which 4 were waited for; matrix products, arithmetic and copies ran while one was open for 3% of the time, Pallas kernels for 0%

commit v1 on v0

--- a/solution.py
+++ b/solution.py
@@ -88,7 +88,7 @@
         summed = jnp.dot(onehot, contrib, precision=lax.Precision.HIGHEST).reshape(
             ALT, EPOCHS, LON_DEV, LAT
         )
-        return lax.psum(summed, "ray")
+        return jnp.sum(lax.all_gather(summed, "ray"), axis=0)
 
     def right_norm_of(values):
         return jnp.sqrt(slab_total(values))

time: 364 us -> 339 us (0.931)
  waiting for transfers between devices: 169 us -> 137 us
  other arithmetic: 29.7 us -> 36.2 us
    psum x2 -> x0, waiting for transfers between devices: 168 us -> none  [pull_back(): return lax.psum(summed, 'ray')]
    all_gather x0 -> x2, waiting for transfers between devices: none -> 132 us  [pull_back(): return jnp.sum(lax.all_gather(summed, 'ray'), axis=0)]
    reduce_sum x0 -> x2, other arithmetic: none -> 8.78 us  [pull_back(): return jnp.sum(lax.all_gather(summed, 'ray'), axis=0)]
    ppermute x3, waiting for transfers between devices: 0.68 us -> 4.74 us  [with_halo(): lax.ppermute(lax.slice_in_dim(block, block.shape[dim] - width, None, axis...]
  transfers between devices with their start and end apart: 8 -> 8, of which waited for: 4 -> 8; matrix products, arithmetic and copies ran while one was open for 3% -> 2% of each run, Pallas kernels for 0% -> 0%
where the time goes in v1:
time: 339 us; the launch traced here: 338 us
  waiting for transfers between devices  137 us (40%)
  blocking collectives  119 us (35%)
  other arithmetic  36.2 us (11%)
  between operations  20 us (6%)
  starting transfers between devices  17.6 us (5%)
  matrix products  5.6 us (2%)
    all_gather x2, waiting for transfers between devices, pull_back(): return jnp.sum(lax.all_gather(summed, 'ray'), axis=0)  132 us
    psum x3, blocking collectives, ray_total(): return lax.psum(jnp.sum(values * values), 'ray')  95.7 us
    ppermute x3, starting transfers between devices, with_halo(): lax.ppermute(lax.slice_in_dim(block, block.shape[dim] - width, None, axis...  13.6 us
    psum x2, blocking collectives, on_device(): ray_sums = lax.psum(partial_value, 'vox')  11.9 us
    psum x2, blocking collectives, slab_total(): return lax.psum(jnp.sum(values * values), 'vox')  11.1 us
    reduce_sum x4, other arithmetic, slab_total(): return lax.psum(jnp.sum(values * values), 'vox')  10.4 us
    reduce_sum x2, other arithmetic, pull_back(): return jnp.sum(lax.all_gather(summed, 'ray'), axis=0)  8.78 us
    concatenate x3, other arithmetic, with_halo(): block = jnp.concatenate([low, block, high], axis=dim)  8.48 us
  transfers between devices with their start and end apart: 8, of which 8 were waited for; matrix products, arithmetic and copies ran while one was open for 2% of the time, Pallas kernels for 0%

profile of v1, /device:TPU:0, one launch (start us, length us, event | category | flops | bytes accessed | tf_op | source)
XLA Modules:
  0.0 338.0 jit_solution(16751635298707591207)
XLA Ops:
  7.2 0.7 compare_select_fusion.1
  8.6 0.8 select_reduce_fusion
  9.5 1.3 multiply_reduce_fusion.5
  10.7 35.5 %psum.63 = f32[]{:T(128)} all-reduce(f32[]{:T(128)} %get-tuple-element.20), channel_id=1, replica_groups=mesh['ray'=16,'vox'=2] {'ray'}, use_global_device_ids=true, to_apply=%region_2.3 | all-reduce | flops 1 | bytes 8 | tf_op jit(solution)/shard_map/psum | solution.py:73
  49.3 1.9 fusion.40
  52.7 71.0 %all-gather.3.cloned.1.call-done = f32[16,64,2,8,128]{4,3,2,1,0:T(8,128)} async-done(((f32[1,64,2,8,128]{4,3,2,1,0:T(8,128)}), f32[16,64,2,8,128]{4,3,2,1,0:T(8,128)}) %all-gather.3.cloned.1.call-update) | async-done | bytes 8388624 | tf_op jit(solution)/shard_map/all_gather | solution.py:91
  123.6 4.0 %reduce_sum.92 = f32[64,2,8,128]{3,2,1,0:T(8,128)S(1)} reduce(f32[16,64,2,8,128]{4,3,2,1,0:T(8,128)} %all-gather.3.cloned.1.call-done, f32[]{:T(128)} %constant.25.clone.1), dimensions={0}, to_apply=%region_3.5 | reduce | flops 1966080 | bytes 8912900 | tf_op jit(solution)/shard_map/reduce_sum | solution.py:91
  127.6 0.7 multiply_reduce_fusion.2
  128.4 5.6 %psum.64 = f32[]{:T(128)} all-reduce(f32[]{:T(128)} %multiply_reduce_fusion.2), channel_id=1, replica_groups=mesh['ray'=16,'vox'=2] {'vox'}, use_global_device_ids=true, to_apply=%region_5.7 | all-reduce | flops 1 | bytes 8 | tf_op jit(solution)/shard_map/psum | solution.py:76
  136.1 1.3 collective-permute-start
  137.4 4.5 %collective-permute-start.1 = (f32[64,2,1,128]{3,2,1,0:T(1,128)S(1)}, f32[64,2,1,128]{3,2,1,0:T(1,128)S(1)}, u32[]{:S(2)}, u32[]{:S(2)}) collective-permute-start(f32[64,2,1,128]{3,2,1,0:T(1,128)S(1)} %get-tuple-element.26), channel_id=1, source_target_pairs={{0,1},{2,3},{4,5},{6,7},{8,9},{10,11},{12,13},{14,15},{16,17},{18,... | collective-permute-start | bytes 196616 | tf_op jit(solution)/shard_map/ppermute | solution.py:23
  142.3 1.6 collective-permute-done.1
  143.8 2.4 select_maximum_fusion.4
  146.2 1.5 multiply_reduce_fusion.1
  147.8 5.9 %all-reduce.4 = (f32[1024]{0:T(1024)S(1)}, f32[]{:T(128)}) all-reduce(f32[1024]{0:T(1024)S(1)} %convolution_bitcast_fusion.1, f32[]{:T(128)} %get-tuple-element.16), channel_id=1, replica_groups=mesh['ray'=16,'vox'=2] {'vox'}, use_global_device_ids=true, to_apply=%region_6.9 | all-reduce | flops 1025 | bytes 8200 | tf_op jit(solution)/shard_map/psum | solution.py:117
  154.3 30.1 %psum.66 = f32[]{:T(128)} all-reduce(f32[]{:T(128)} %get-tuple-element.14), channel_id=1, replica_groups=mesh['ray'=16,'vox'=2] {'ray'}, use_global_device_ids=true, to_apply=%region_8.11 | all-reduce | flops 1 | bytes 8 | tf_op jit(solution)/shard_map/psum | solution.py:73
  186.8 1.3 fusion.39
  188.3 1.3 collective-permute-start.2
  189.6 4.5 %collective-permute-start.3 = (f32[64,2,1,128]{3,2,1,0:T(1,128)S(1)}, f32[64,2,1,128]{3,2,1,0:T(1,128)S(1)}, u32[]{:S(2)}, u32[]{:S(2)}) collective-permute-start(f32[64,2,1,128]{3,2,1,0:T(1,128)S(1)} %get-tuple-element.24), channel_id=1, source_target_pairs={{0,1},{2,3},{4,5},{6,7},{8,9},{10,11},{12,13},{14,15},{16,17},{18,... | collective-permute-start | bytes 196616 | tf_op jit(solution)/shard_map/ppermute | solution.py:23
  194.5 1.6 collective-permute-done.3
  196.1 3.7 %select_maximum_fusion.2 = f32[66,4,10,130]{3,2,1,0:T(8,128)} fusion(f32[64,2,1,128]{3,2,1,0:T(1,128)S(1)} %collective-permute-done.2, f32[64,2,8,128]{3,2,1,0:T(8,128)S(1)} %broadcast_multiply_fusion, f32[64,2,1,128]{3,2,1,0:T(1,128)S(1)} %collective-permute-done.3), kind=kLoop, calls=%fused_computation.12 | loop fusion | flops 7550400 | bytes 2028160 | tf_op jit(solution)/shard_map/concatenate | solution.py:27
  199.8 61.2 %all-gather.5.cloned.1.call-done = f32[16,64,2,8,128]{4,3,2,1,0:T(8,128)} async-done(((f32[1,64,2,8,128]{4,3,2,1,0:T(8,128)}), f32[16,64,2,8,128]{4,3,2,1,0:T(8,128)}) %all-gather.5.cloned.1.call-update) | async-done | bytes 8388624 | tf_op jit(solution)/shard_map/all_gather | solution.py:91
  261.0 4.8 %reduce_sum.96 = f32[64,2,8,128]{3,2,1,0:T(8,128)} reduce(f32[16,64,2,8,128]{4,3,2,1,0:T(8,128)} %all-gather.5.cloned.1.call-done, f32[]{:T(128)} %constant.25.clone.1), dimensions={0}, to_apply=%region_11.14 | reduce | flops 1966080 | bytes 8912900 | tf_op jit(solution)/shard_map/reduce_sum | solution.py:91
  265.8 6.6 %multiply_reduce_fusion = (f32[]{:T(128)}, f32[64,2,8,128]{3,2,1,0:T(8,128)S(1)}) fusion(f32[64,2,8,128]{3,2,1,0:T(8,128)S(1)} %get-tuple-element.19, f32[]{:T(128)S(6)} %sqrt.23, f32[64,2,8,128]{3,2,1,0:T(8,128)} %reduce_sum.96, f32[66,4,10,130]{3,2,1,0:T(8,128)} %select_maximum_fusion.2, f32[64,2,8,128]{3,2,1,0:T(8,128)S(1)} %broadcast_multiply_fusion, ...), kind=kLoop, calls=%fused_computation.75 | loop fusion | flops 2359295 | bytes 5373960 | tf_op jit(solution)/shard_map/reduce_sum | solution.py:76
  272.3 5.5 %psum.68 = f32[]{:T(128)} all-reduce(f32[]{:T(128)} %get-tuple-element.12), channel_id=1, replica_groups=mesh['ray'=16,'vox'=2] {'vox'}, use_global_device_ids=true, to_apply=%region_13.16 | all-reduce | flops 1 | bytes 8 | tf_op jit(solution)/shard_map/psum | solution.py:76
  280.1 1.3 collective-permute-start.4
  281.4 4.5 %collective-permute-start.5 = (f32[64,2,1,128]{3,2,1,0:T(1,128)S(1)}, f32[64,2,1,128]{3,2,1,0:T(1,128)S(1)}, u32[]{:S(2)}, u32[]{:S(2)}) collective-permute-start(f32[64,2,1,128]{3,2,1,0:T(1,128)S(1)} %get-tuple-element.22), channel_id=1, source_target_pairs={{0,1},{2,3},{4,5},{6,7},{8,9},{10,11},{12,13},{14,15},{16,17},{18,... | collective-permute-start | bytes 196616 | tf_op jit(solution)/shard_map/ppermute | solution.py:23
  286.2 1.6 collective-permute-done.5
  287.8 2.4 select_maximum_fusion
  290.2 1.6 fusion.18
  291.8 5.9 %all-reduce.3 = (f32[1024]{0:T(1024)S(1)}, f32[]{:T(128)}) all-reduce(f32[1024]{0:T(1024)S(1)} %convolution_bitcast_fusion, f32[]{:T(128)} %fusion.18), channel_id=1, replica_groups=mesh['ray'=16,'vox'=2] {'vox'}, use_global_device_ids=true, to_apply=%region_14.17 | all-reduce | flops 1025 | bytes 8200 | tf_op jit(solution)/shard_map/psum | solution.py:117
  298.3 30.1 %psum.70 = f32[]{:T(128)} all-reduce(f32[]{:T(128)} %get-tuple-element.8), channel_id=1, replica_groups=mesh['ray'=16,'vox'=2] {'ray'}, use_global_device_ids=true, to_apply=%region_16.19 | all-reduce | flops 1 | bytes 8 | tf_op jit(solution)/shard_map/psum | solution.py:73
  (47 shorter events, 11.2 us)
Async XLA Ops:
  7.2 41.1 %copy-start = (bf16[1,1,32,128,128]{4,3,2,1,0:T(8,128)(2,1)S(1)}, bf16[1,1,32,128,128]{4,3,2,1,0:T(8,128)(2,1)}, u32[]{:S(2)}) copy-start(bf16[1,1,32,128,128]{4,3,2,1,0:T(8,128)(2,1)} %param.13) | copy-start | bytes 3145732
  7.2 116.5 %all-gather.3.cloned.1.call-start = ((), (), s32[]{:S(2)}) async-start(), calls=%async_computation | async-start | bytes 8912896 | tf_op jit(solution)/shard_map/all_gather | solution.py:91
  51.3 209.7 %all-gather.5.cloned.1.call-start = ((), (), s32[]{:S(2)}) async-start(), calls=%async_computation.1 | async-start | bytes 8912896 | tf_op jit(solution)/shard_map/all_gather | solution.py:91
  52.7 89.3 %copy-start.3 = (s32[1,1,32]{2,1,0:T(1,128)S(1)}, s32[1,1,32]{2,1,0:T(1,128)}, u32[]{:S(2)}) copy-start(s32[1,1,32]{2,1,0:T(1,128)} %param.15) | copy-start | bytes 388
  127.6 18.6 %copy-start.1 = (f32[64]{0:T(128)S(1)}, f32[64]{0:T(128)}, u32[]{:S(2)}) copy-start(f32[64]{0:T(128)} %param.21) | copy-start | bytes 772
  136.1 6.2 %collective-permute-start = (f32[64,2,1,128]{3,2,1,0:T(1,128)S(1)}, f32[64,2,1,128]{3,2,1,0:T(1,128)S(1)}, u32[]{:S(2)}, u32[]{:S(2)}) collective-permute-start(f32[64,2,1,128]{3,2,1,0:T(1,128)S(1)} %get-tuple-element.27), channel_id=1, source_target_pairs={{1,0},{3,2},{5,4},{7,6},{9,8},{11,10},{13,12},{15,14},{17,16},{19,... | collective-permute-start | bytes 196616 | tf_op jit(solution)/shard_map/ppermute | solution.py:26
  137.4 6.4 %collective-permute-start.1 = (f32[64,2,1,128]{3,2,1,0:T(1,128)S(1)}, f32[64,2,1,128]{3,2,1,0:T(1,128)S(1)}, u32[]{:S(2)}, u32[]{:S(2)}) collective-permute-start(f32[64,2,1,128]{3,2,1,0:T(1,128)S(1)} %get-tuple-element.26), channel_id=1, source_target_pairs={{0,1},{2,3},{4,5},{6,7},{8,9},{10,11},{12,13},{14,15},{16,17},{18,... | collective-permute-start | bytes 196616 | tf_op jit(solution)/shard_map/ppermute | solution.py:23
  142.2 44.6 %copy-start.2 = (s32[1,1,32]{2,1,0:T(1,128)S(1)}, s32[1,1,32]{2,1,0:T(1,128)}, u32[]{:S(2)}) copy-start(s32[1,1,32]{2,1,0:T(1,128)} %param.16) | copy-start | bytes 388
  188.3 6.2 %collective-permute-start.2 = (f32[64,2,1,128]{3,2,1,0:T(1,128)S(1)}, f32[64,2,1,128]{3,2,1,0:T(1,128)S(1)}, u32[]{:S(2)}, u32[]{:S(2)}) collective-permute-start(f32[64,2,1,128]{3,2,1,0:T(1,128)S(1)} %get-tuple-element.25), channel_id=1, source_target_pairs={{1,0},{3,2},{5,4},{7,6},{9,8},{11,10},{13,12},{15,14},{17,16},{19,... | collective-permute-start | bytes 196616 | tf_op jit(solution)/shard_map/ppermute | solution.py:26
  189.6 6.4 %collective-permute-start.3 = (f32[64,2,1,128]{3,2,1,0:T(1,128)S(1)}, f32[64,2,1,128]{3,2,1,0:T(1,128)S(1)}, u32[]{:S(2)}, u32[]{:S(2)}) collective-permute-start(f32[64,2,1,128]{3,2,1,0:T(1,128)S(1)} %get-tuple-element.24), channel_id=1, source_target_pairs={{0,1},{2,3},{4,5},{6,7},{8,9},{10,11},{12,13},{14,15},{16,17},{18,... | collective-permute-start | bytes 196616 | tf_op jit(solution)/shard_map/ppermute | solution.py:23
  280.1 6.2 %collective-permute-start.4 = (f32[64,2,1,128]{3,2,1,0:T(1,128)S(1)}, f32[64,2,1,128]{3,2,1,0:T(1,128)S(1)}, u32[]{:S(2)}, u32[]{:S(2)}) collective-permute-start(f32[64,2,1,128]{3,2,1,0:T(1,128)S(1)} %get-tuple-element.23), channel_id=1, source_target_pairs={{1,0},{3,2},{5,4},{7,6},{9,8},{11,10},{13,12},{15,14},{17,16},{19,... | collective-permute-start | bytes 196616 | tf_op jit(solution)/shard_map/ppermute | solution.py:26
  281.4 6.4 %collective-permute-start.5 = (f32[64,2,1,128]{3,2,1,0:T(1,128)S(1)}, f32[64,2,1,128]{3,2,1,0:T(1,128)S(1)}, u32[]{:S(2)}, u32[]{:S(2)}) collective-permute-start(f32[64,2,1,128]{3,2,1,0:T(1,128)S(1)} %get-tuple-element.22), channel_id=1, source_target_pairs={{0,1},{2,3},{4,5},{6,7},{8,9},{10,11},{12,13},{14,15},{16,17},{18,... | collective-permute-start | bytes 196616 | tf_op jit(solution)/shard_map/ppermute | solution.py:23
Sparse Core Ops, SparseCore 0:
  51.4 72.1 all-gather.2
  188.2 72.6 all-gather.4
